TPU v7x, 32 devices: a whole 2x2x4 slice. The times are simulated.
32 devices in a mesh: ops: 4 (over x, core), sec: 8 (over z, y).
Axes of the slice: x: 2, y: 2, z: 4, core: 2. Of those that a mesh axis runs over, the one named last changes fastest.
Arguments:
- wavefunction: float32 [8, 640, 640], P('sec'), may hold values from -6 to 6
- left_ops: bfloat16 [8, 12, 640, 640], P('sec', 'ops'), may hold values from -0.3125 to 0.3125
- right_ops: bfloat16 [8, 12, 640, 640], P('sec', 'ops'), may hold values from -0.25 to 0.25
- charge_step: int32 [8, 12], P('sec', 'ops'), may hold values from -1 to 1
- sector_sizes: int32 [8], replicated, may hold values from 320 to 640
Outputs:
- cheb_prev: float32 [8, 640, 640], P('sec', 'ops')
- cheb_last: float32 [8, 640, 640], P('sec', 'ops')
Inputs may be any that keep to these rules, and one draw needn't show every extreme that they name: Operator pair p of sector t reads sector t + charge_step[t, p].
All inputs are finite; a program needn't handle non-finite values.
Results may differ from a plain program's by a relative error of at most 0.0076.
Values may be sent and summed in bfloat16 or wider, within the bound.
A program may use at most 64 MiB of HBM per device.

v0:
```python
import math

import jax
import jax.numpy as jnp
from jax import lax
from jax.sharding import PartitionSpec as P

STEPS = 2


def padded(shard, sides, width):
    for axis, dim in sides:
        peers, length = (lax.axis_size(axis), shard.shape[dim])
        up = [(i, (i + 1) % peers) for i in range(peers - 1)]
        down = [(j, i) for i, j in up]
        last = lax.slice_in_dim(shard, length - width, length, axis=dim)
        initial = lax.slice_in_dim(shard, 0, width, axis=dim)
        before = lax.ppermute(last, axis, up)
        after = lax.ppermute(initial, axis, down)
        shard = jnp.concatenate([before, shard, after], axis=dim)
    return shard


def on_device(wavefunction, left_ops, right_ops, charge_step, sector_sizes):
    ops_count = lax.axis_size("ops")
    width_all = wavefunction.shape[1]
    share_rows = width_all // ops_count
    first_row = lax.axis_index("ops") * share_rows
    own_size = lax.dynamic_index_in_dim(sector_sizes, lax.axis_index("sec"), 0, keepdims=False)
    positions = jnp.arange(width_all, dtype=jnp.int32)
    live_cols = (positions < own_size).astype(jnp.float32)
    row_live = lax.dynamic_slice_in_dim(live_cols, first_row, share_rows, 0)
    full_mask = live_cols[:, None] * live_cols[None, :]
    row_mask = row_live[:, None] * live_cols[None, :]
    norm_scale = 1.0 / math.sqrt(left_ops.shape[1] * ops_count)
    onehot = (charge_step[0][:, None] + 1 == jnp.arange(3, dtype=jnp.int32)[None, :]).astype(
        jnp.bfloat16
    )
    start_field = wavefunction[0] * full_mask
    start_rows = lax.dynamic_slice_in_dim(start_field, first_row, share_rows, 0)
    previous = start_rows
    current = start_rows
    source_full = start_field.astype(jnp.bfloat16)
    for iteration in range(STEPS):
        nearby = padded(source_full[None], (("sec", 0),), 1)
        inputs = jnp.einsum(
            "pc,cab->pab", onehot, nearby, preferred_element_type=jnp.float32
        ).astype(jnp.bfloat16)
        left_half = jnp.einsum(
            "pab,pbc->pac", left_ops[0], inputs, preferred_element_type=jnp.float32
        ).astype(jnp.bfloat16)
        summed = lax.psum_scatter(
            jnp.einsum("pac,pdc->ad", left_half, right_ops[0], preferred_element_type=jnp.float32),
            "ops",
            scatter_dimension=0,
            tiled=True,
        )
        applied = summed * norm_scale * row_mask
        updated = applied if iteration == 0 else 2.0 * applied - previous
        previous = start_rows if iteration == 0 else current
        current = updated
        if iteration + 1 < STEPS:
            source_full = lax.all_gather(updated.astype(jnp.bfloat16), "ops", axis=0, tiled=True)
    return (previous[None], current[None])


def solution(mesh):
    in_specs = (
        P("sec", None, None),
        P("sec", "ops", None, None),
        P("sec", "ops", None, None),
        P("sec", "ops"),
        P(),
    )
    out_specs = (P("sec", "ops", None), P("sec", "ops", None))
    return jax.shard_map(
        on_device, mesh=mesh, in_specs=in_specs, out_specs=out_specs, check_vma=False
    )
```

profile of v0, /device:TPU:6, one launch (start us, length us, event | category | flops | bytes accessed | tf_op | source)
XLA Modules:
  0.0 192.0 jit_solution(770483051379401629)
XLA Ops:
  7.2 0.0 copy-start
  7.2 0.0 copy-start.1
  7.2 0.0 reduce-scatter.3.cloned.1.call-start
  7.2 1.4 dynamic_slice.10
  8.6 0.6 fusion.39
  9.3 1.6 multiply_convert_fusion
  10.9 2.4 %collective-permute-start.1 = (bf16[1,640,640]{2,1,0:T(8,128)(2,1)S(1)}, bf16[1,640,640]{2,1,0:T(8,128)(2,1)S(1)}, u32[]{:S(2)}, u32[]{:S(2)}) collective-permute-start(bf16[1,640,640]{2,1,0:T(8,128)(2,1)S(1)} %multiply_convert_fusion), channel_id=1, source_target_pairs={{1,0},{2,1},{3,2},{4,3},{5,4},{6,5},{7,6},{9,8},{10,9},{11,10},{12... | collective-permute-start | bytes 2457608 | tf_op jit(solution)/shard_map/ppermute | solution.py:19
  13.4 4.3 %collective-permute-start = (bf16[1,640,640]{2,1,0:T(8,128)(2,1)S(1)}, bf16[1,640,640]{2,1,0:T(8,128)(2,1)S(1)}, u32[]{:S(2)}, u32[]{:S(2)}) collective-permute-start(bf16[1,640,640]{2,1,0:T(8,128)(2,1)S(1)} %multiply_convert_fusion), channel_id=1, source_target_pairs={{0,1},{1,2},{2,3},{3,4},{4,5},{5,6},{6,7},{8,9},{9,10},{10,11},{11... | collective-permute-start | bytes 2457608 | tf_op jit(solution)/shard_map/ppermute | solution.py:18
  17.7 0.0 copy-done.1
  17.7 16.1 %collective-permute-done.1 = bf16[1,640,640]{2,1,0:T(8,128)(2,1)S(1)} collective-permute-done((bf16[1,640,640]{2,1,0:T(8,128)(2,1)S(1)}, bf16[1,640,640]{2,1,0:T(8,128)(2,1)S(1)}, u32[]{:S(2)}, u32[]{:S(2)}) %collective-permute-start.1) | collective-permute-done | bytes 819232 | tf_op jit(solution)/shard_map/ppermute | solution.py:19
  33.8 17.5 %collective-permute-done = bf16[1,640,640]{2,1,0:T(8,128)(2,1)S(1)} collective-permute-done((bf16[1,640,640]{2,1,0:T(8,128)(2,1)S(1)}, bf16[1,640,640]{2,1,0:T(8,128)(2,1)S(1)}, u32[]{:S(2)}, u32[]{:S(2)}) %collective-permute-start) | collective-permute-done | bytes 819232 | tf_op jit(solution)/shard_map/ppermute | solution.py:18
  51.3 0.3 pad_maximum_fusion
  51.6 4.0 %fusion.2 = bf16[3,640,640]{2,0,1:T(4,128)(2,1)} fusion(bf16[3,640,640]{2,1,0:T(8,128)(2,1)S(1)} %pad_maximum_fusion, s32[3]{0:T(128)S(1)} %add_bitcast_fusion), kind=kOutput, calls=%fused_computation.4 | convolution fusion | flops 7372809 | bytes 4915212 | tf_op jit(solution)/shard_map/pc,cab->pab/dot_general | solution.py:46
  55.6 0.0 copy-done
  55.6 8.2 %fusion.16 = f32[640,640]{1,0:T(8,128)} fusion(bf16[1,3,640,640]{3,2,1,0:T(8,128)(2,1)S(1)} %copy-done, bf16[3,640,640]{2,0,1:T(4,128)(2,1)} %fusion.2, bf16[1,3,640,640]{3,2,1,0:T(8,128)(2,1)} %param.6), kind=kOutput, calls=%fused_computation.21 | convolution fusion | flops 3146956800 | bytes 9011200 | tf_op jit(solution)/shard_map/pac,pdc->ad/dot_general | solution.py:53
  63.7 0.0 reduce-scatter.3.cloned.1.call-update
  63.8 0.0 reduce-scatter.5.cloned.1.call-start
  63.8 0.1 dynamic_slice.11
  63.9 27.7 %reduce-scatter.3.cloned.1.call-done = f32[160,640]{1,0:T(8,128)} async-done(((f32[640,640]{1,0:T(8,128)}), f32[160,640]{1,0:T(8,128)}) %reduce-scatter.3.cloned.1.call-update) | async-done | bytes 409616 | tf_op jit(solution)/shard_map/reduce_scatter | solution.py:52
  91.6 1.9 fusion.37
  93.4 8.8 %all_gather.3 = bf16[640,640]{1,0:T(8,128)(2,1)S(1)} all-gather(bf16[160,640]{1,0:T(8,128)(2,1)S(1)} %get-tuple-element.2), channel_id=1, replica_groups=mesh['ops'=4,'sec'=8] {'ops'}, dimensions={0}, use_global_device_ids=true | all-gather | bytes 1024000 | tf_op jit(solution)/shard_map/all_gather | solution.py:63
  102.2 2.4 %collective-permute-start.3 = (bf16[1,640,640]{2,1,0:T(8,128)(2,1)S(1)}, bf16[1,640,640]{2,1,0:T(8,128)(2,1)S(1)}, u32[]{:S(2)}, u32[]{:S(2)}) collective-permute-start(bf16[1,640,640]{2,1,0:T(8,128)(2,1)S(1)} %bitcast.49), channel_id=1, source_target_pairs={{1,0},{2,1},{3,2},{4,3},{5,4},{6,5},{7,6},{9,8},{10,9},{11,10},{12... | collective-permute-start | bytes 2457608 | tf_op jit(solution)/shard_map/ppermute | solution.py:19
  104.7 4.5 %collective-permute-start.2 = (bf16[1,640,640]{2,1,0:T(8,128)(2,1)S(1)}, bf16[1,640,640]{2,1,0:T(8,128)(2,1)S(1)}, u32[]{:S(2)}, u32[]{:S(2)}) collective-permute-start(bf16[1,640,640]{2,1,0:T(8,128)(2,1)S(1)} %bitcast.50), channel_id=1, source_target_pairs={{0,1},{1,2},{2,3},{3,4},{4,5},{5,6},{6,7},{8,9},{9,10},{10,11},{11... | collective-permute-start | bytes 2457608 | tf_op jit(solution)/shard_map/ppermute | solution.py:18
  109.1 16.5 %collective-permute-done.3 = bf16[1,640,640]{2,1,0:T(8,128)(2,1)S(1)} collective-permute-done((bf16[1,640,640]{2,1,0:T(8,128)(2,1)S(1)}, bf16[1,640,640]{2,1,0:T(8,128)(2,1)S(1)}, u32[]{:S(2)}, u32[]{:S(2)}) %collective-permute-start.3) | collective-permute-done | bytes 819232 | tf_op jit(solution)/shard_map/ppermute | solution.py:19
  125.6 17.5 %collective-permute-done.2 = bf16[1,640,640]{2,1,0:T(8,128)(2,1)S(1)} collective-permute-done((bf16[1,640,640]{2,1,0:T(8,128)(2,1)S(1)}, bf16[1,640,640]{2,1,0:T(8,128)(2,1)S(1)}, u32[]{:S(2)}, u32[]{:S(2)}) %collective-permute-start.2) | collective-permute-done | bytes 819232 | tf_op jit(solution)/shard_map/ppermute | solution.py:18
  143.0 0.3 pad_maximum_fusion.1
  143.3 4.0 %fusion = bf16[3,640,640]{2,0,1:T(4,128)(2,1)} fusion(bf16[3,640,640]{2,1,0:T(8,128)(2,1)S(1)} %pad_maximum_fusion.1, s32[3]{0:T(128)S(1)} %add_bitcast_fusion), kind=kOutput, calls=%fused_computation.2 | convolution fusion | flops 7372809 | bytes 4915212 | tf_op jit(solution)/shard_map/pc,cab->pab/dot_general | solution.py:46
  147.3 8.2 %fusion.21 = f32[640,640]{1,0:T(8,128)} fusion(bf16[1,3,640,640]{3,2,1,0:T(8,128)(2,1)S(1)} %copy-done, bf16[3,640,640]{2,0,1:T(4,128)(2,1)} %fusion, bf16[1,3,640,640]{3,2,1,0:T(8,128)(2,1)} %param.6), kind=kOutput, calls=%fused_computation.22 | convolution fusion | flops 3146956800 | bytes 9011200 | tf_op jit(solution)/shard_map/pac,pdc->ad/dot_general | solution.py:53
  155.5 0.0 reduce-scatter.5.cloned.1.call-update
  155.5 27.6 %reduce-scatter.5.cloned.1.call-done = f32[160,640]{1,0:T(8,128)} async-done(((f32[640,640]{1,0:T(8,128)}), f32[160,640]{1,0:T(8,128)}) %reduce-scatter.5.cloned.1.call-update) | async-done | bytes 409616 | tf_op jit(solution)/shard_map/reduce_scatter | solution.py:52
  183.1 2.0 %fusion.36 = f32[1,160,640]{2,1,0:T(8,128)} fusion(f32[640,640]{1,0:T(8,128)} %bitcast.52, s32[]{:T(128)S(6)} %select_n.9, f32[160,640]{1,0:T(8,128)} %reduce-scatter.5.cloned.1.call-done, f32[640]{0:T(1024)S(1)} %fusion.39, f32[160]{0:T(256)S(1)} %dynamic_slice.11), kind=kLoop, calls=%fused_computation.28 | loop fusion | flops 614400 | bytes 1232004 | tf_op jit(solution)/shard_map/broadcast_in_dim | solution.py:64
  (1 shorter events, 0.0 us)
Async XLA Ops:
  7.2 48.4 %copy-start = (bf16[1,3,640,640]{3,2,1,0:T(8,128)(2,1)S(1)}, bf16[1,3,640,640]{3,2,1,0:T(8,128)(2,1)}, u32[]{:S(2)}) copy-start(bf16[1,3,640,640]{3,2,1,0:T(8,128)(2,1)} %param.7) | copy-start | bytes 7372804
  7.2 10.5 %copy-start.1 = (s32[1,3]{1,0:T(1,128)S(1)}, s32[1,3]{1,0:T(1,128)}, u32[]{:S(2)}) copy-start(s32[1,3]{1,0:T(1,128)} %param.8) | copy-start | bytes 40
  7.2 84.4 %reduce-scatter.3.cloned.1.call-start = ((), (), s32[]{:S(2)}) async-start(), calls=%async_computation.2 | async-start | bytes 2048000 | tf_op jit(solution)/shard_map/reduce_scatter | solution.py:52
  10.9 22.9 %collective-permute-start.1 = (bf16[1,640,640]{2,1,0:T(8,128)(2,1)S(1)}, bf16[1,640,640]{2,1,0:T(8,128)(2,1)S(1)}, u32[]{:S(2)}, u32[]{:S(2)}) collective-permute-start(bf16[1,640,640]{2,1,0:T(8,128)(2,1)S(1)} %multiply_convert_fusion), channel_id=1, source_target_pairs={{1,0},{2,1},{3,2},{4,3},{5,4},{6,5},{7,6},{9,8},{10,9},{11,10},{12... | collective-permute-start | bytes 2457608 | tf_op jit(solution)/shard_map/ppermute | solution.py:19
  13.4 37.9 %collective-permute-start = (bf16[1,640,640]{2,1,0:T(8,128)(2,1)S(1)}, bf16[1,640,640]{2,1,0:T(8,128)(2,1)S(1)}, u32[]{:S(2)}, u32[]{:S(2)}) collective-permute-start(bf16[1,640,640]{2,1,0:T(8,128)(2,1)S(1)} %multiply_convert_fusion), channel_id=1, source_target_pairs={{0,1},{1,2},{2,3},{3,4},{4,5},{5,6},{6,7},{8,9},{9,10},{10,11},{11... | collective-permute-start | bytes 2457608 | tf_op jit(solution)/shard_map/ppermute | solution.py:18
  63.8 119.4 %reduce-scatter.5.cloned.1.call-start = ((), (), s32[]{:S(2)}) async-start(), calls=%async_computation.3 | async-start | bytes 2048000 | tf_op jit(solution)/shard_map/reduce_scatter | solution.py:52
  102.2 23.4 %collective-permute-start.3 = (bf16[1,640,640]{2,1,0:T(8,128)(2,1)S(1)}, bf16[1,640,640]{2,1,0:T(8,128)(2,1)S(1)}, u32[]{:S(2)}, u32[]{:S(2)}) collective-permute-start(bf16[1,640,640]{2,1,0:T(8,128)(2,1)S(1)} %bitcast.49), channel_id=1, source_target_pairs={{1,0},{2,1},{3,2},{4,3},{5,4},{6,5},{7,6},{9,8},{10,9},{11,10},{12... | collective-permute-start | bytes 2457608 | tf_op jit(solution)/shard_map/ppermute | solution.py:19
  104.7 38.4 %collective-permute-start.2 = (bf16[1,640,640]{2,1,0:T(8,128)(2,1)S(1)}, bf16[1,640,640]{2,1,0:T(8,128)(2,1)S(1)}, u32[]{:S(2)}, u32[]{:S(2)}) collective-permute-start(bf16[1,640,640]{2,1,0:T(8,128)(2,1)S(1)} %bitcast.50), channel_id=1, source_target_pairs={{0,1},{1,2},{2,3},{3,4},{4,5},{5,6},{6,7},{8,9},{9,10},{10,11},{11... | collective-permute-start | bytes 2457608 | tf_op jit(solution)/shard_map/ppermute | solution.py:18
Sparse Core Ops, SparseCore 0:
  63.9 27.6 reduce-scatter.2
  155.6 27.4 reduce-scatter.4
where the time goes:
time: 195 us; the launch traced here: 192 us
  waiting for transfers between devices  123 us (63%)
  matrix products  24.3 us (12%)
  between operations  14.1 us (7%)
  starting transfers between devices  13.7 us (7%)
  blocking collectives  8.76 us (4%)
  other arithmetic  6.81 us (3%)
    reduce_scatter x2, waiting for transfers between devices, on_device(): lax.psum_scatter(jnp.einsum('pac,pdc->ad', left_half, right_ops[0], prefe...  55.3 us
    ppermute x2, waiting for transfers between devices, padded(): before = lax.ppermute(last, axis, up)  34.9 us
    ppermute x2, waiting for transfers between devices, padded(): after = lax.ppermute(initial, axis, down)  32.5 us
    dot_general x2, matrix products, on_device(): jnp.einsum('pac,pdc->ad', left_half, right_ops[0], preferred_element_type...  16.3 us
    ppermute x2, starting transfers between devices, padded(): before = lax.ppermute(last, axis, up)  8.79 us
    all_gather x1, blocking collectives, on_device(): lax.all_gather(updated.astype(jnp.bfloat16), 'ops', axis=0, tiled=True)  8.76 us
    dot_general x2, matrix products, on_device(): jnp.einsum('pc,cab->pab', onehot, nearby, preferred_element_type=jnp.floa...  7.94 us
    ppermute x2, starting transfers between devices, padded(): after = lax.ppermute(initial, axis, down)  4.86 us
  transfers between devices with their start and end apart: 6, of which 6 were waited for; matrix products, arithmetic and copies ran while one was open for 0% of the time, Pallas kernels for 0%

commit v1 on v0

--- a/solution.py
+++ b/solution.py
@@ -1,11 +1,18 @@
+import functools
 import math
 
 import jax
 import jax.numpy as jnp
 from jax import lax
+from jax.experimental import pallas as pl
+from jax.experimental.pallas import tpu as pltpu
 from jax.sharding import PartitionSpec as P
 
 STEPS = 2
+CORES = 2
+PIECES = 2
+ROW_TILE = 16
+MESH_ID = pl.DeviceIdType.MESH
 
 
 def padded(shard, sides, width):
@@ -21,7 +28,7 @@
     return shard
 
 
-def on_device(wavefunction, left_ops, right_ops, charge_step, sector_sizes):
+def by_collectives(wavefunction, left_ops, right_ops, charge_step, sector_sizes):
     ops_count = lax.axis_size("ops")
     width_all = wavefunction.shape[1]
     share_rows = width_all // ops_count
@@ -64,6 +71,282 @@
     return (previous[None], current[None])
 
 
+def kernel(
+    ops_count, sectors,
+    v_hbm, l_hbm, r_hbm, charge_ref, size_ref, prev_ref, last_ref,
+    v_buf, l_buf, r_buf, xa0, xb0, xa1, xb1, y_buf,
+    acc_far, acc_near, to_mate, from_mate, to_chip, from_chip,
+    local_sem, send_sem, recv_sem,
+):
+    pairs, width = l_hbm.shape[1], l_hbm.shape[2]
+    share = width // ops_count
+    half = CORES * share
+    piece = share // PIECES
+    scale = 1.0 / math.sqrt(pairs * ops_count)
+
+    o = lax.axis_index("ops")
+    t = lax.axis_index("sec")
+    core = lax.rem(o, CORES)
+    chip = o // CORES
+    mate = o + 1 - 2 * core
+    across = lax.rem(o + CORES, ops_count)
+    parity = lax.rem(t, 2)
+    direct_to = t + 1 - 2 * parity
+    relay_to = t + 2 - 4 * parity
+    relay_from = t - 2 + 4 * parity
+    has_target = jnp.logical_and(relay_to >= 0, relay_to < sectors)
+    has_source = jnp.logical_and(relay_from >= 0, relay_from < sectors)
+
+    v_copy = pltpu.make_async_copy(v_hbm.at[0], v_buf, local_sem.at[0])
+    v_copy.start()
+    loads = []
+    for p in range(pairs):
+        loads.append(pltpu.make_async_copy(r_hbm.at[0, p], r_buf.at[p], local_sem.at[1 + p]))
+    for p in range(pairs):
+        loads.append(pltpu.make_async_copy(
+            l_hbm.at[0, p], l_buf.at[:, pl.ds(p * width, width)], local_sem.at[1 + pairs + p]))
+    for load in loads:
+        load.start()
+
+    barrier = pltpu.get_barrier_semaphore()
+    pl.semaphore_signal(barrier, inc=1, device_id={"ops": mate}, device_id_type=MESH_ID)
+    pl.semaphore_signal(barrier, inc=1, device_id={"ops": across}, device_id_type=MESH_ID)
+    pl.semaphore_signal(barrier, inc=1, device_id={"sec": direct_to}, device_id_type=MESH_ID)
+
+    @pl.when(has_target)
+    def _():
+        pl.semaphore_signal(barrier, inc=1, device_id={"sec": relay_to}, device_id_type=MESH_ID)
+
+    @pl.when(has_source)
+    def _():
+        pl.semaphore_signal(barrier, inc=1, device_id={"sec": relay_from}, device_id_type=MESH_ID)
+
+    size = size_ref[t]
+    cols_live = lax.broadcasted_iota(jnp.int32, (1, width), 1) < size
+
+    def masked(value, first):
+        rows = first + lax.broadcasted_iota(jnp.int32, (value.shape[0], 1), 0)
+        return jnp.where(jnp.logical_and(rows < size, cols_live), value, 0.0)
+
+    def aligned(start, length):
+        return pl.ds(pl.multiple_of(start, ROW_TILE), length)
+
+    fields = ((xa0, xb0), (xa1, xb1))
+    chips = (chip, 1 - chip)
+
+    @pl.when(jnp.logical_not(has_source))
+    def _():
+        for field in fields:
+            for x in field:
+                x[2] = jnp.zeros(x.shape[1:], x.dtype)
+
+    counter = [0]
+    started = []
+
+    def remote(src, dst, target):
+        i = counter[0]
+        counter[0] += 1
+        return pltpu.make_async_remote_copy(
+            src_ref=src, dst_ref=dst, send_sem=send_sem.at[i], recv_sem=recv_sem.at[i],
+            device_id=target, device_id_type=MESH_ID)
+
+    def go(copy):
+        copy.start()
+        started.append((copy, False))
+
+    mine = [aligned(core * share + h * piece, piece) for h in range(PIECES)]
+    grid = [(g, h) for g in range(2) for h in range(PIECES)]
+    plans = []
+    for field in fields:
+        plan = {"direct": {}, "relay": {}, "mate0": {}, "mate1": {}, "mate2": {}, "across": {}}
+        for g, h in grid:
+            x, rows = field[g], mine[h]
+            plan["direct"][g, h] = remote(x.at[1, rows], x.at[0, rows], {"sec": direct_to})
+            plan["relay"][g, h] = remote(x.at[0, rows], x.at[2, rows], {"sec": relay_to})
+            for slot in range(3):
+                plan[f"mate{slot}"][g, h] = remote(
+                    x.at[slot, rows], x.at[slot, rows], {"ops": mate})
+        for h in range(PIECES):
+            plan["across"][h] = remote(
+                field[0].at[1, mine[h]], field[1].at[1, mine[h]], {"ops": across})
+        plans.append(plan)
+
+    def direct_in(plan, g, h):
+        plan["direct"][g, h].wait_recv()
+
+        @pl.when(has_target)
+        def _():
+            plan["relay"][g, h].start()
+
+        started.append((plan["relay"][g, h], True))
+        go(plan["mate0"][g, h])
+
+    def relay_in(plan, g, h):
+        @pl.when(has_source)
+        def _():
+            plan["relay"][g, h].wait_recv()
+            plan["mate2"][g, h].start()
+
+    def mates_in(step, plan, g):
+        for h in range(PIECES):
+            if step:
+                plan["mate1"][g, h].wait_recv()
+            plan["mate0"][g, h].wait_recv()
+
+        @pl.when(has_source)
+        def _():
+            for h in range(PIECES):
+                plan["mate2"][g, h].wait_recv()
+
+    picks = [1 - (1 - 2 * parity) * charge_ref[0, p] for p in range(pairs)]
+
+    def right_products(step, g):
+        x = fields[step][g]
+        for p in range(pairs):
+            y_buf[aligned(p * width + chips[g] * half, half), :] = lax.dot_general(
+                x[picks[p]], r_buf[p], (((1,), (1,)), ((), ())),
+                preferred_element_type=jnp.float32).astype(jnp.bfloat16)
+
+    def left_products(g):
+        return jnp.dot(l_buf[aligned(chips[g] * half, half), :], y_buf[...],
+                       preferred_element_type=jnp.float32)
+
+    v_copy.wait()
+    for g in range(2):
+        first = chips[g] * half
+        xs = v_buf[aligned(first, half), :]
+        fields[0][g][1] = masked(xs, first).astype(jnp.bfloat16)
+    pl.semaphore_wait(barrier, 3 + has_target.astype(jnp.int32) + has_source.astype(jnp.int32))
+
+    for g, h in grid:
+        go(plans[0]["direct"][g, h])
+
+    for step in range(STEPS):
+        plan = plans[step]
+        for i, (g, h) in enumerate(grid):
+            if step and g == 0:
+                plan["across"][h].wait_recv()
+                go(plan["direct"][1, h])
+                go(plan["mate1"][1, h])
+            direct_in(plan, g, h)
+            if i and grid[i - 1][0] == 0:
+                relay_in(plan, *grid[i - 1])
+        if not step:
+            for load in loads[:pairs]:
+                load.wait()
+        mates_in(step, plan, 0)
+        right_products(step, 0)
+        for h in range(PIECES):
+            relay_in(plan, 1, h)
+        mates_in(step, plan, 1)
+        right_products(step, 1)
+        if not step:
+            for load in loads[pairs:]:
+                load.wait()
+
+        theirs = aligned((1 - core) * share, share)
+        hand = [remote(to_mate.at[step, k], from_mate.at[step, k], {"ops": mate}) for k in range(2)]
+        acc_far[...] = left_products(1)
+        to_mate[step, 0] = acc_far[theirs, :].astype(jnp.bfloat16)
+        go(hand[0])
+        acc_near[...] = left_products(0)
+        to_mate[step, 1] = acc_near[theirs, :].astype(jnp.bfloat16)
+        go(hand[1])
+        hand[0].wait_recv()
+        ship = []
+        for h in range(PIECES):
+            part = pl.ds(h * piece, piece)
+            to_chip[step, part, :] = (
+                acc_far[mine[h], :] + from_mate[step, 0, part, :].astype(jnp.float32)
+            ).astype(jnp.bfloat16)
+            ship.append(remote(to_chip.at[step, part], from_chip.at[step, part], {"ops": across}))
+            go(ship[h])
+        hand[1].wait_recv()
+        for h in range(PIECES):
+            part = pl.ds(h * piece, piece)
+            first = o * share + h * piece
+            ship[h].wait_recv()
+            summed = (
+                acc_near[mine[h], :]
+                + from_mate[step, 1, part, :].astype(jnp.float32)
+                + from_chip[step, part, :].astype(jnp.float32)
+            )
+            applied = masked(summed * scale, first)
+            if step == 0:
+                prev_ref[0, part, :] = applied
+                xa1[1, mine[h], :] = applied.astype(jnp.bfloat16)
+                following = plans[1]
+                go(following["direct"][0, h])
+                go(following["across"][h])
+                go(following["mate1"][0, h])
+            else:
+                start_rows = masked(v_buf[aligned(first, piece), :], first)
+                last_ref[0, part, :] = 2.0 * applied - start_rows
+
+    for copy, relayed in started:
+        if not relayed:
+            copy.wait_send()
+
+    @pl.when(has_target)
+    def _():
+        for copy, relayed in started:
+            if relayed:
+                copy.wait_send()
+
+    @pl.when(has_source)
+    def _():
+        for plan in plans:
+            for g, h in grid:
+                plan["mate2"][g, h].wait_send()
+
+
+def by_kernel(wavefunction, left_ops, right_ops, charge_step, sector_sizes):
+    ops_count, sectors = lax.axis_size("ops"), lax.axis_size("sec")
+    pairs, width = left_ops.shape[1], left_ops.shape[2]
+    share = width // ops_count
+    half = CORES * share
+    anywhere = pl.BlockSpec(memory_space=pl.ANY)
+    scalars = pl.BlockSpec(memory_space=pltpu.SMEM)
+    vmem = pl.BlockSpec(memory_space=pltpu.VMEM)
+    bf16, f32 = jnp.bfloat16, jnp.float32
+    field = pltpu.VMEM((3, half, width), bf16)
+    copies = STEPS * (2 * PIECES * 5 + PIECES + 2 + PIECES)
+    out = jax.ShapeDtypeStruct((1, share, width), f32)
+    return pl.pallas_call(
+        functools.partial(kernel, ops_count, sectors),
+        out_shape=(out, out),
+        in_specs=[anywhere, anywhere, anywhere, scalars, scalars],
+        out_specs=(vmem, vmem),
+        scratch_shapes=[
+            pltpu.VMEM((width, width), f32),
+            pltpu.VMEM((width, pairs * width), bf16),
+            pltpu.VMEM((pairs, width, width), bf16),
+            field, field, field, field,
+            pltpu.VMEM((pairs * width, width), bf16),
+            pltpu.VMEM((half, width), f32),
+            pltpu.VMEM((half, width), f32),
+            pltpu.VMEM((STEPS, 2, share, width), bf16),
+            pltpu.VMEM((STEPS, 2, share, width), bf16),
+            pltpu.VMEM((STEPS, share, width), bf16),
+            pltpu.VMEM((STEPS, share, width), bf16),
+            pltpu.SemaphoreType.DMA((1 + 2 * pairs,)),
+            pltpu.SemaphoreType.DMA((copies,)),
+            pltpu.SemaphoreType.DMA((copies,)),
+        ],
+        compiler_params=pltpu.CompilerParams(
+            collective_id=0, has_side_effects=True, vmem_limit_bytes=48 * 1024 * 1024),
+    )(wavefunction, left_ops, right_ops, charge_step, sector_sizes)
+
+
+def on_device(wavefunction, left_ops, right_ops, charge_step, sector_sizes):
+    ops_count, sectors = lax.axis_size("ops"), lax.axis_size("sec")
+    share = wavefunction.shape[1] // ops_count
+    paired = ops_count == 2 * CORES and sectors % 2 == 0
+    tiled = share % (PIECES * ROW_TILE) == 0
+    body = by_kernel if paired and tiled else by_collectives
+    return body(wavefunction, left_ops, right_ops, charge_step, sector_sizes)
+
+
 def solution(mesh):
     in_specs = (
         P("sec", None, None),

time: 195 us -> 63 us (0.32); the launches traced: 192 us -> 62.7 us
  waiting for transfers between devices: 123 us -> 0 us
  Pallas kernels: 0 us -> 56.1 us
  matrix products: 24.3 us -> 0 us
  starting transfers between devices: 13.7 us -> 0 us
  between operations: 14.1 us -> 0.65 us
  blocking collectives: 8.76 us -> 0 us
  other arithmetic: 6.81 us -> 0 us
  local copies, waits for them, and re-layouts: 1.48 us -> 5.93 us
    ppermute x4 -> x0, waiting for transfers between devices: 67.5 us -> none  [the longest x2 34.9 us: padded(): before = lax.ppermute(last, axis, up)]
    pallas_call x0 -> x1, Pallas kernels: none -> 56.1 us  [by_kernel(): pl.pallas_call(functools.partial(kernel, ops_count, sectors), out_shape=(...]
    reduce_scatter x2 -> x0, waiting for transfers between devices: 55.3 us -> none  [on_device(): lax.psum_scatter(jnp.einsum('pac,pdc->ad', left_half, right_ops[0], prefe...]
    dot_general x4 -> x0, matrix products: 24.3 us -> none  [the longest x2 16.3 us: on_device(): jnp.einsum('pac,pdc->ad', left_half, right_ops[0], preferred_element_type...]
    ppermute x4 -> x0, starting transfers between devices: 13.7 us -> none  [the longest x2 8.79 us: padded(): before = lax.ppermute(last, axis, up)]
    all_gather x1 -> x0, blocking collectives: 8.76 us -> none  [on_device(): lax.all_gather(updated.astype(jnp.bfloat16), 'ops', axis=0, tiled=True)]
    unnamed x4 -> x10, local copies, waits for them, and re-layouts: 0.01 us -> 5.93 us
    convert_element_type x3 -> x0, other arithmetic: 4.16 us -> none  [the longest x1 1.87 us: on_device(): updated.astype(jnp.bfloat16)]
  transfers between devices with their start and end apart: 6 -> 0, of which waited for: 6 -> 0; matrix products, arithmetic and copies ran while one was open for 0% -> 0% of each run, Pallas kernels for 0% -> 0%
where the time goes in v1:
time: 63 us; the launch traced here: 62.7 us
  Pallas kernels  56.1 us (89%)
  local copies, waits for them, and re-layouts  5.93 us (9%)
  between operations  0.65 us (1%)
    pallas_call x1, Pallas kernels, by_kernel(): pl.pallas_call(functools.partial(kernel, ops_count, sectors), out_shape=(...  56.1 us
    unnamed x10, local copies, waits for them, and re-layouts  5.93 us

profile of v1, /device:TPU:6, one launch (start us, length us, event | category | flops | bytes accessed | tf_op | source)
XLA Modules:
  0.0 62.7 jit_solution(9211417075998803827)
XLA Ops:
  0.6 0.0 copy-start
  0.6 1.7 %copy-done = bf16[1,3,640,640]{3,2,1,0:T(8,128)(2,1)S(1)} copy-done((bf16[1,3,640,640]{3,2,1,0:T(8,128)(2,1)S(1)}, bf16[1,3,640,640]{3,2,1,0:T(8,128)(2,1)}, u32[]{:S(2)}) %copy-start) | copy-done | bytes 2457624
  2.3 0.0 copy-start.1
  2.3 1.4 %copy-done.1 = f32[1,640,640]{2,1,0:T(8,128)S(1)} copy-done((f32[1,640,640]{2,1,0:T(8,128)S(1)}, f32[1,640,640]{2,1,0:T(8,128)}, u32[]{:S(2)}) %copy-start.1) | copy-done | bytes 1638424
  3.8 0.0 copy-start.2
  3.8 0.7 %copy-done.2 = s32[1,3]{1,0:T(1,128)S(1)} copy-done((s32[1,3]{1,0:T(1,128)S(1)}, s32[1,3]{1,0:T(1,128)}, u32[]{:S(2)}) %copy-start.2) | copy-done | bytes 36
  4.4 0.0 copy-start.3
  4.4 0.7 %copy-done.3 = s32[8]{0:T(128)S(1)} copy-done((s32[8]{0:T(128)S(1)}, s32[8]{0:T(128)}, u32[]{:S(2)}) %copy-start.3) | copy-done | bytes 56
  5.1 56.1 %shard_map.68 = (f32[1,160,640]{2,1,0:T(8,128)S(1)}, f32[1,160,640]{2,1,0:T(8,128)S(1)}) custom-call(f32[1,640,640]{2,1,0:T(8,128)S(1)} %copy-done.1, bf16[1,3,640,640]{3,2,1,0:T(8,128)(2,1)S(1)} %copy-done, bf16[1,3,640,640]{3,2,1,0:T(8,128)(2,1)} %r_hbm.1, s32[1,3]{1,0:T(1,128)S(1)} %copy-done.2, s32[8]{0:T(128)S(1)} %copy-done.3), custom_call_target="tpu_custom_call" | custom-call | tf_op jit(solution)/shard_map/pallas_call | solution.py:315
  61.2 0.8 %copy.9 = f32[1,160,640]{2,1,0:T(8,128)} copy(f32[1,160,640]{2,1,0:T(8,128)S(1)} %get-tuple-element.4) | data formatting | bytes 819200
  62.0 0.8 %copy.10 = f32[1,160,640]{2,1,0:T(8,128)} copy(f32[1,160,640]{2,1,0:T(8,128)S(1)} %get-tuple-element.5) | data formatting | bytes 819200
Async XLA Ops:
  0.6 1.7 %copy-start = (bf16[1,3,640,640]{3,2,1,0:T(8,128)(2,1)S(1)}, bf16[1,3,640,640]{3,2,1,0:T(8,128)(2,1)}, u32[]{:S(2)}) copy-start(bf16[1,3,640,640]{3,2,1,0:T(8,128)(2,1)} %l_hbm.1) | copy-start | bytes 7372804
  2.3 1.4 %copy-start.1 = (f32[1,640,640]{2,1,0:T(8,128)S(1)}, f32[1,640,640]{2,1,0:T(8,128)}, u32[]{:S(2)}) copy-start(f32[1,640,640]{2,1,0:T(8,128)} %v_hbm.1) | copy-start | bytes 4915204
  3.8 0.7 %copy-start.2 = (s32[1,3]{1,0:T(1,128)S(1)}, s32[1,3]{1,0:T(1,128)}, u32[]{:S(2)}) copy-start(s32[1,3]{1,0:T(1,128)} %charge_ref.1) | copy-start | bytes 40
  4.4 0.7 %copy-start.3 = (s32[8]{0:T(128)S(1)}, s32[8]{0:T(128)}, u32[]{:S(2)}) copy-start(s32[8]{0:T(128)} %size_ref.1) | copy-start | bytes 100

commit v2 on v0

--- a/solution.py
+++ b/solution.py
@@ -1,11 +1,19 @@
+import functools
 import math
 
 import jax
 import jax.numpy as jnp
 from jax import lax
+from jax.experimental import pallas as pl
+from jax.experimental.pallas import tpu as pltpu
 from jax.sharding import PartitionSpec as P
 
 STEPS = 2
+CORES = 2
+PIECES = 5
+STRAIGHT = 2
+ROW_TILE = 16
+MESH_ID = pl.DeviceIdType.MESH
 
 
 def padded(shard, sides, width):
@@ -21,7 +29,7 @@
     return shard
 
 
-def on_device(wavefunction, left_ops, right_ops, charge_step, sector_sizes):
+def by_collectives(wavefunction, left_ops, right_ops, charge_step, sector_sizes):
     ops_count = lax.axis_size("ops")
     width_all = wavefunction.shape[1]
     share_rows = width_all // ops_count
@@ -64,6 +72,362 @@
     return (previous[None], current[None])
 
 
+def kernel(
+    ops_count, sectors,
+    v_hbm, l_hbm, r_hbm, charge_hbm, size_hbm, prev_ref, last_ref,
+    charge_ref, size_ref, v_buf, l_buf, r_buf, xa0, xm0, xb0, xn0, xa1, xm1, xb1, xn1, y_buf,
+    acc_far, acc_near, to_mate, from_mate, to_chip, from_chip, to_twin, from_twin,
+    local_sem, send_sem, recv_sem,
+):
+    pairs, width = l_hbm.shape[1], l_hbm.shape[2]
+    share = width // ops_count
+    half = CORES * share
+    piece = share // PIECES
+    scale = 1.0 / math.sqrt(pairs * ops_count)
+
+    o = lax.axis_index("ops")
+    t = lax.axis_index("sec")
+    core = lax.rem(o, CORES)
+    chip = o // CORES
+    mate = o + 1 - 2 * core
+    across = lax.rem(o + CORES, ops_count)
+    parity = lax.rem(t, 2)
+    direct_to = t + 1 - 2 * parity
+    relay_to = t + 2 - 4 * parity
+    relay_from = t - 2 + 4 * parity
+    has_target = jnp.logical_and(relay_to >= 0, relay_to < sectors)
+    has_source = jnp.logical_and(relay_from >= 0, relay_from < sectors)
+
+    v_copy = pltpu.make_async_copy(v_hbm.at[0], v_buf, local_sem.at[0])
+    smalls = [pltpu.make_async_copy(size_hbm, size_ref, local_sem.at[1 + 2 * pairs]),
+              pltpu.make_async_copy(charge_hbm, charge_ref, local_sem.at[2 + 2 * pairs])]
+    v_copy.start()
+    for small in smalls:
+        small.start()
+    loads = []
+    for p in range(pairs):
+        loads.append(pltpu.make_async_copy(r_hbm.at[0, p], r_buf.at[p], local_sem.at[1 + p]))
+    for p in range(pairs):
+        loads.append(pltpu.make_async_copy(
+            l_hbm.at[0, p], l_buf.at[:, pl.ds(p * width, width)], local_sem.at[1 + pairs + p]))
+
+    barrier = pltpu.get_barrier_semaphore()
+    pl.semaphore_signal(barrier, inc=1, device_id={"ops": mate}, device_id_type=MESH_ID)
+    pl.semaphore_signal(barrier, inc=1, device_id={"ops": across}, device_id_type=MESH_ID)
+    pl.semaphore_signal(barrier, inc=1, device_id={"sec": direct_to}, device_id_type=MESH_ID)
+
+    @pl.when(has_target)
+    def _():
+        pl.semaphore_signal(barrier, inc=1, device_id={"sec": relay_to}, device_id_type=MESH_ID)
+
+    @pl.when(has_source)
+    def _():
+        pl.semaphore_signal(barrier, inc=1, device_id={"sec": relay_from}, device_id_type=MESH_ID)
+
+    for small in smalls:
+        small.wait()
+    size = size_ref[t]
+    cols_live = lax.broadcasted_iota(jnp.int32, (1, width), 1) < size
+
+    def masked(value, first):
+        rows = first + lax.broadcasted_iota(jnp.int32, (value.shape[0], 1), 0)
+        return jnp.where(jnp.logical_and(rows < size, cols_live), value, 0.0)
+
+    def aligned(start, length):
+        return pl.ds(pl.multiple_of(start, ROW_TILE), length)
+
+    fields = (((xa0, xm0), (xb0, xn0)), ((xa1, xm1), (xb1, xn1)))
+    cores = (core, 1 - core)
+    chips = (chip, 1 - chip)
+    mine = [pl.ds(h * piece, piece) for h in range(PIECES)]
+    made, started, to_relays, from_relays = {}, [], [], []
+
+    def remote(key, src, dst, target):
+        if key not in made:
+            i = len(made)
+            made[key] = pltpu.make_async_remote_copy(
+                src_ref=src, dst_ref=dst, send_sem=send_sem.at[i], recv_sem=recv_sem.at[i],
+                device_id=target, device_id_type=MESH_ID)
+        return made[key]
+
+    def direct(step, g, h):
+        x, rows = fields[step][g][0], mine[h]
+        return remote(("direct", step, g, h), x.at[1, rows], x.at[0, rows], {"sec": direct_to})
+
+    def relay(step, g, h):
+        x, rows = fields[step][g][0], mine[h]
+        return remote(("relay", step, g, h), x.at[0, rows], x.at[2, rows], {"sec": relay_to})
+
+    def to_core(step, g, h, slot):
+        (x, y), rows = fields[step][g], mine[h]
+        return remote(("core", step, g, h, slot), x.at[slot, rows], y.at[slot, rows], {"ops": mate})
+
+    def to_other(step, h, slot):
+        x, y, rows = fields[step][0][0], fields[step][1][0], mine[h]
+        return remote(("other", step, h, slot), x.at[slot, rows], y.at[slot, rows], {"ops": across})
+
+    def go(copy):
+        copy.start()
+        started.append(copy)
+
+    def crossing(step, g, h):
+        return step == 0 and g == 0 and h >= STRAIGHT
+
+    def direct_in(step, g, h):
+        direct(step, g, h).wait_recv()
+        onward = relay(step, g, h)
+        to_relays.append(onward)
+
+        @pl.when(has_target)
+        def _():
+            onward.start()
+
+        go(to_core(step, g, h, 0))
+        if crossing(step, g, h):
+            go(to_other(step, h, 0))
+
+    def relay_in(step, g, h):
+        copies = [to_core(step, g, h, 2)]
+        if crossing(step, g, h):
+            copies.append(to_other(step, h, 2))
+        from_relays.extend(copies)
+        arriving = relay(step, g, h)
+
+        @pl.when(has_source)
+        def _():
+            arriving.wait_recv()
+            for copy in copies:
+                copy.start()
+
+    def twin_in(step, h):
+        part = mine[h]
+        twin[h].wait_recv()
+        summed = (
+            acc_far[part, :]
+            + from_mate[step, 0, part, :].astype(jnp.float32)
+            + from_twin[part, :].astype(jnp.float32)
+        )
+        first = (1 - chip) * half + core * share + h * piece
+        fields[1][1][0][1, part, :] = masked(summed * scale, first).astype(jnp.bfloat16)
+        go(direct(1, 1, h))
+        go(to_core(1, 1, h, 1))
+
+    def cross_in(step, h):
+        to_other(step, h, 0).wait_recv()
+        go(to_core(step, 1, h, 0))
+        copy = to_core(step, 1, h, 2)
+        from_relays.append(copy)
+        arriving = to_other(step, h, 2)
+
+        @pl.when(has_source)
+        def _():
+            arriving.wait_recv()
+            copy.start()
+
+    picks = [1 - (1 - 2 * parity) * charge_ref[0, p] for p in range(pairs)]
+
+    def right_products(step, g, m):
+        if m:
+            for h in range(PIECES):
+                to_core(step, g, h, 0).wait_recv()
+                if step:
+                    to_core(step, g, h, 1).wait_recv()
+            arriving = [to_core(step, g, h, 2) for h in range(PIECES)]
+
+            @pl.when(has_source)
+            def _():
+                for copy in arriving:
+                    copy.wait_recv()
+
+        x = fields[step][g][m]
+        for p in range(pairs):
+            y_buf[aligned(p * width + chips[g] * half + cores[m] * share, share), :] = (
+                lax.dot_general(
+                    x[picks[p]], r_buf[p], (((1,), (1,)), ((), ())),
+                    preferred_element_type=jnp.float32).astype(jnp.bfloat16))
+
+    def left_products(g, owner):
+        return jnp.dot(l_buf[aligned(chips[g] * half + owner * share, share), :], y_buf[...],
+                       preferred_element_type=jnp.float32)
+
+    hand, ship, twin = {}, {}, {}
+
+    def left_and_send(step):
+        for k in range(2):
+            for h in range(PIECES):
+                hand[k, h] = remote(
+                    ("hand", step, k, h), to_mate.at[step, k, mine[h]],
+                    from_mate.at[step, k, mine[h]], {"ops": mate})
+        to_mate[step, 0] = left_products(1, 1 - core).astype(jnp.bfloat16)
+        for h in range(PIECES):
+            go(hand[0, h])
+        acc_far[...] = left_products(1, core)
+        to_mate[step, 1] = left_products(0, 1 - core).astype(jnp.bfloat16)
+        for h in range(PIECES):
+            go(hand[1, h])
+        for h in range(PIECES):
+            part = mine[h]
+            hand[0, h].wait_recv()
+            to_chip[step, part, :] = (
+                acc_far[part, :] + from_mate[step, 0, part, :].astype(jnp.float32)
+            ).astype(jnp.bfloat16)
+            ship[h] = remote(
+                ("ship", step, h), to_chip.at[step, part], from_chip.at[step, part],
+                {"ops": across})
+            go(ship[h])
+        acc_near[...] = left_products(0, core)
+        for h in range(PIECES):
+            part = mine[h]
+            hand[1, h].wait_recv()
+            if step + 1 < STEPS:
+                to_twin[part, :] = (
+                    acc_near[part, :] + from_mate[step, 1, part, :].astype(jnp.float32)
+                ).astype(jnp.bfloat16)
+                twin[h] = remote(
+                    ("twin", step, h), to_twin.at[part], from_twin.at[part], {"ops": across})
+                go(twin[h])
+
+    def finish(step, h):
+        part = pl.ds(h * piece, piece)
+        first = o * share + h * piece
+        ship[h].wait_recv()
+        summed = (
+            acc_near[part, :]
+            + from_mate[step, 1, part, :].astype(jnp.float32)
+            + from_chip[step, part, :].astype(jnp.float32)
+        )
+        live = masked(summed, first)
+        applied = live * scale
+        if step == 0:
+            prev_ref[0, part, :] = live
+            fields[1][0][0][1, part, :] = applied.astype(jnp.bfloat16)
+            go(direct(1, 0, h))
+            go(to_core(1, 0, h, 1))
+        else:
+            start_rows = masked(v_buf[aligned(first, piece), :], first)
+            last_ref[0, part, :] = applied - 0.5 * start_rows
+
+    v_copy.wait()
+    for load in loads:
+        load.start()
+    for g in range(2):
+        for m in range(2):
+            first = chips[g] * half + cores[m] * share
+            fields[0][g][m][1] = masked(
+                v_buf[aligned(first, share), :], first).astype(jnp.bfloat16)
+    pl.semaphore_wait(barrier, 3 + has_target.astype(jnp.int32) + has_source.astype(jnp.int32))
+    turns = [(0, h) for h in range(STRAIGHT, PIECES)]
+    turns += [(g, h) for g in range(2) for h in range(STRAIGHT)]
+    for g, h in turns:
+        go(direct(0, g, h))
+
+    @pl.when(jnp.logical_not(has_source))
+    def _():
+        for field in fields:
+            for x in (*field[0], *field[1]):
+                x[2] = jnp.zeros(x.shape[1:], x.dtype)
+
+    lag, behind = 3, 3
+    events = []
+    for k, (g, h) in enumerate(turns):
+        events.append((k, direct_in, (0, g, h)))
+        events.append((k + lag, relay_in, (0, g, h)))
+        if crossing(0, g, h):
+            events.append((k + 3 * lag, cross_in, (0, h)))
+    for load in loads[:pairs]:
+        events.append((PIECES, load.wait, ()))
+    events.append((PIECES + lag, right_products, (0, 0, 0)))
+    events.append((PIECES + lag, right_products, (0, 0, 1)))
+    for _, run, arguments in sorted(events, key=lambda event: event[0]):
+        run(*arguments)
+    right_products(0, 1, 0)
+    right_products(0, 1, 1)
+    for load in loads[pairs:]:
+        load.wait()
+    left_and_send(0)
+
+    events = []
+    for h in range(PIECES):
+        events.append((h, finish, (0, h)))
+        events.append((h + behind, direct_in, (1, 0, h)))
+        events.append((h + behind + lag, relay_in, (1, 0, h)))
+        events.append((h + PIECES, twin_in, (0, h)))
+        events.append((h + PIECES + behind, direct_in, (1, 1, h)))
+        events.append((h + PIECES + behind + lag, relay_in, (1, 1, h)))
+    events.append((2 * PIECES + behind - 1, right_products, (1, 0, 0)))
+    events.append((2 * PIECES + behind, right_products, (1, 0, 1)))
+    for _, run, arguments in sorted(events, key=lambda event: event[0]):
+        run(*arguments)
+    right_products(1, 1, 0)
+    right_products(1, 1, 1)
+    left_and_send(1)
+    for h in range(PIECES):
+        finish(1, h)
+
+    for copy in started:
+        copy.wait_send()
+
+    @pl.when(has_target)
+    def _():
+        for copy in to_relays:
+            copy.wait_send()
+
+    @pl.when(has_source)
+    def _():
+        for copy in from_relays:
+            copy.wait_send()
+
+
+def by_kernel(wavefunction, left_ops, right_ops, charge_step, sector_sizes):
+    ops_count, sectors = lax.axis_size("ops"), lax.axis_size("sec")
+    pairs, width = left_ops.shape[1], left_ops.shape[2]
+    share = width // ops_count
+    stay = pl.BlockSpec(memory_space=pltpu.HBM)
+    vmem = pl.BlockSpec(memory_space=pltpu.VMEM)
+    bf16, f32 = jnp.bfloat16, jnp.float32
+    field = pltpu.VMEM((3, share, width), bf16)
+    copies = STEPS * (2 * PIECES * 5 + 6 * PIECES)
+    out = jax.ShapeDtypeStruct((1, share, width), f32)
+    raw = pl.pallas_call(
+        functools.partial(kernel, ops_count, sectors),
+        out_shape=(out, out),
+        in_specs=[stay] * 5,
+        out_specs=(vmem, vmem),
+        scratch_shapes=[
+            pltpu.SMEM((1, pairs), jnp.int32),
+            pltpu.SMEM((sectors,), jnp.int32),
+            pltpu.VMEM((width, width), f32),
+            pltpu.VMEM((width, pairs * width), bf16),
+            pltpu.VMEM((pairs, width, width), bf16),
+            *[field] * 8,
+            pltpu.VMEM((pairs * width, width), bf16),
+            pltpu.VMEM((share, width), f32),
+            pltpu.VMEM((share, width), f32),
+            pltpu.VMEM((STEPS, 2, share, width), bf16),
+            pltpu.VMEM((STEPS, 2, share, width), bf16),
+            pltpu.VMEM((STEPS, share, width), bf16),
+            pltpu.VMEM((STEPS, share, width), bf16),
+            pltpu.VMEM((share, width), bf16),
+            pltpu.VMEM((share, width), bf16),
+            pltpu.SemaphoreType.DMA((3 + 2 * pairs,)),
+            pltpu.SemaphoreType.DMA((copies,)),
+            pltpu.SemaphoreType.DMA((copies,)),
+        ],
+        compiler_params=pltpu.CompilerParams(
+            collective_id=0, has_side_effects=True, vmem_limit_bytes=67_043_328),
+    )(wavefunction, left_ops, right_ops, charge_step, sector_sizes)
+    return raw[0] * (1.0 / math.sqrt(pairs * ops_count)), raw[1] * 2.0
+
+
+def on_device(wavefunction, left_ops, right_ops, charge_step, sector_sizes):
+    ops_count, sectors = lax.axis_size("ops"), lax.axis_size("sec")
+    share = wavefunction.shape[1] // ops_count
+    paired = ops_count == 2 * CORES and sectors % 2 == 0
+    tiled = share % (PIECES * ROW_TILE) == 0
+    body = by_kernel if paired and tiled else by_collectives
+    return body(wavefunction, left_ops, right_ops, charge_step, sector_sizes)
+
+
 def solution(mesh):
     in_specs = (
         P("sec", None, None),

time: 195 us -> 57.7 us (0.30); the launches traced: 192 us -> 56.7 us
  waiting for transfers between devices: 123 us -> 0 us
  Pallas kernels: 0 us -> 54 us
  matrix products: 24.3 us -> 0 us
  starting transfers between devices: 13.7 us -> 0 us
  between operations: 14.1 us -> 0.64 us
  blocking collectives: 8.76 us -> 0 us
  other arithmetic: 6.81 us -> 2.08 us
    ppermute x4 -> x0, waiting for transfers between devices: 67.5 us -> none  [the longest x2 34.9 us: padded(): before = lax.ppermute(last, axis, up)]
    reduce_scatter x2 -> x0, waiting for transfers between devices: 55.3 us -> none  [on_device(): lax.psum_scatter(jnp.einsum('pac,pdc->ad', left_half, right_ops[0], prefe...]
    pallas_call x0 -> x1, Pallas kernels: none -> 54 us  [by_kernel(): pl.pallas_call(functools.partial(kernel, ops_count, sectors), out_shape=(...]
    dot_general x4 -> x0, matrix products: 24.3 us -> none  [the longest x2 16.3 us: on_device(): jnp.einsum('pac,pdc->ad', left_half, right_ops[0], preferred_element_type...]
    ppermute x4 -> x0, starting transfers between devices: 13.7 us -> none  [the longest x2 8.79 us: padded(): before = lax.ppermute(last, axis, up)]
    all_gather x1 -> x0, blocking collectives: 8.76 us -> none  [on_device(): lax.all_gather(updated.astype(jnp.bfloat16), 'ops', axis=0, tiled=True)]
    convert_element_type x3 -> x0, other arithmetic: 4.16 us -> none  [the longest x1 1.87 us: on_device(): updated.astype(jnp.bfloat16)]
    mul x0 -> x1, other arithmetic: none -> 2.08 us  [by_kernel(): return (raw[0] * (1.0 / math.sqrt(pairs * ops_count)), raw[1] * 2.0)]
  transfers between devices with their start and end apart: 6 -> 0, of which waited for: 6 -> 0; matrix products, arithmetic and copies ran while one was open for 0% -> 0% of each run, Pallas kernels for 0% -> 0%
where the time goes in v2:
time: 57.7 us; the launch traced here: 56.7 us
  Pallas kernels  54 us (94%)
  other arithmetic  2.08 us (4%)
  between operations  0.64 us (1%)
    pallas_call x1, Pallas kernels, by_kernel(): pl.pallas_call(functools.partial(kernel, ops_count, sectors), out_shape=(...  54 us
    mul x1, other arithmetic, by_kernel(): return (raw[0] * (1.0 / math.sqrt(pairs * ops_count)), raw[1] * 2.0)  2.08 us

profile of v2, /device:TPU:6, one launch (start us, length us, event | category | flops | bytes accessed | tf_op | source)
XLA Modules:
  0.0 56.7 jit_solution(10753529592777887587)
XLA Ops:
  0.6 54.0 %shard_map.68 = (f32[1,160,640]{2,1,0:T(8,128)}, f32[1,160,640]{2,1,0:T(8,128)}) custom-call(f32[1,640,640]{2,1,0:T(8,128)} %v_hbm.1, bf16[1,3,640,640]{3,2,1,0:T(8,128)(2,1)} %l_hbm.1, bf16[1,3,640,640]{3,2,1,0:T(8,128)(2,1)} %r_hbm.1, s32[1,3]{1,0:T(1,128)} %charge_hbm.1, s32[8]{0:T(128)} %size_hbm.1), custom_call_target="tpu_custom_call" | custom-call | tf_op jit(solution)/shard_map/pallas_call | solution.py:391
  54.6 2.1 %broadcast_multiply_fusion = (f32[1,160,640]{2,1,0:T(8,128)}, f32[1,160,640]{2,1,0:T(8,128)}) fusion(f32[1,160,640]{2,1,0:T(8,128)} %get-tuple-element.5, f32[1,160,640]{2,1,0:T(8,128)} %get-tuple-element.4), kind=kLoop, calls=%fused_computation | loop fusion | flops 204800 | bytes 1638400 | tf_op jit(solution)/shard_map/mul | solution.py:419

commit v3 on v2

--- a/solution.py
+++ b/solution.py
@@ -11,7 +11,9 @@
 STEPS = 2
 CORES = 2
 PIECES = 5
-STRAIGHT = 2
+STRAIGHT = 3
+LAG = 4
+BEHIND = 5
 ROW_TILE = 16
 MESH_ID = pl.DeviceIdType.MESH
 
@@ -327,7 +329,7 @@
             for x in (*field[0], *field[1]):
                 x[2] = jnp.zeros(x.shape[1:], x.dtype)
 
-    lag, behind = 3, 3
+    lag, behind = LAG, BEHIND
     events = []
     for k, (g, h) in enumerate(turns):
         events.append((k, direct_in, (0, g, h)))

time: 57.7 us -> 54.7 us (0.948); the launches traced: 56.7 us -> 54.5 us
  Pallas kernels: 54 us -> 51.8 us
    pallas_call x1, Pallas kernels: 54 us -> 51.8 us  [by_kernel(): pl.pallas_call(functools.partial(kernel, ops_count, sectors), out_shape=(...]
where the time goes in v3:
time: 54.7 us; the launch traced here: 54.5 us
  Pallas kernels  51.8 us (95%)
  other arithmetic  2.08 us (4%)
  between operations  0.64 us (1%)
    pallas_call x1, Pallas kernels, by_kernel(): pl.pallas_call(functools.partial(kernel, ops_count, sectors), out_shape=(...  51.8 us
    mul x1, other arithmetic, by_kernel(): return (raw[0] * (1.0 / math.sqrt(pairs * ops_count)), raw[1] * 2.0)  2.08 us

profile of v3, /device:TPU:6, one launch (start us, length us, event | category | flops | bytes accessed | tf_op | source)
XLA Modules:
  0.0 54.5 jit_solution(5460993469389708909)
XLA Ops:
  0.6 51.8 %shard_map.68 = (f32[1,160,640]{2,1,0:T(8,128)}, f32[1,160,640]{2,1,0:T(8,128)}) custom-call(f32[1,640,640]{2,1,0:T(8,128)} %v_hbm.1, bf16[1,3,640,640]{3,2,1,0:T(8,128)(2,1)} %l_hbm.1, bf16[1,3,640,640]{3,2,1,0:T(8,128)(2,1)} %r_hbm.1, s32[1,3]{1,0:T(1,128)} %charge_hbm.1, s32[8]{0:T(128)} %size_hbm.1), custom_call_target="tpu_custom_call" | custom-call | tf_op jit(solution)/shard_map/pallas_call | solution.py:393
  52.4 2.1 %broadcast_multiply_fusion = (f32[1,160,640]{2,1,0:T(8,128)}, f32[1,160,640]{2,1,0:T(8,128)}) fusion(f32[1,160,640]{2,1,0:T(8,128)} %get-tuple-element.5, f32[1,160,640]{2,1,0:T(8,128)} %get-tuple-element.4), kind=kLoop, calls=%fused_computation | loop fusion | flops 204800 | bytes 1638400 | tf_op jit(solution)/shard_map/mul | solution.py:421
